TPU v7x, 32 devices: a whole 2x2x4 slice. The times are simulated.
32 devices in a mesh: groups: 1, wide: 8 (over y, x, core), narrow: 4 (over z).
Axes of the slice: x: 2, y: 2, z: 4, core: 2. Of those that a mesh axis runs over, the one named last changes fastest.
Arguments:
- table_cells: bfloat16 [128, 128, 192], P(('groups', 'wide', 'narrow')), may hold values from -12 to 12
- counts: int32 [128], P(('groups', 'wide', 'narrow')), may hold values from 32 to 128, as said below
- train_count: int32 [1], P('groups'), may hold values from 32 to 96
- norm_gain: float32 [3, 192], replicated, may hold values from 0.5 to 1.5
- feature_in: bfloat16 [192, 576], P('narrow'), may hold values from -0.4375 to 0.4375
- feature_out: bfloat16 [192, 192], P('narrow'), may hold values from -0.4375 to 0.4375
- sample_in: bfloat16 [192, 576], P('narrow'), may hold values from -0.4375 to 0.4375
- sample_out: bfloat16 [192, 192], P('narrow'), may hold values from -0.4375 to 0.4375
- hidden_up: bfloat16 [192, 768], P('narrow'), may hold values from -0.4375 to 0.4375
- hidden_down: bfloat16 [768, 192], P('narrow'), may hold values from -0.21875 to 0.21875
Outputs:
- updated_cells: bfloat16 [128, 128, 192], P(('groups', 'wide', 'narrow'))
Inputs may be any that keep to these rules, and one draw needn't show every extreme that they name: `counts`: feature j of a row is present when j < its count; some row has all 128 features present. Rows 0 to train_count - 1 are the training rows.
All inputs are finite; a program needn't handle non-finite values.
Results may differ from a plain program's by a relative error of at most 0.0086.
Values may be sent and summed in bfloat16 or wider, within the bound.
A program may use at most 64 MiB of HBM per device.

v0:
```python
import jax
import jax.numpy as jnp
from jax import lax
from jax.sharding import PartitionSpec as P

HEADS = 6


epsilon = 1e-05


def normalize(values, gain):
    average = jnp.mean(values, axis=-1, keepdims=True)
    centered = values - average
    spread = jnp.mean(centered * centered, axis=-1, keepdims=True)
    return centered * lax.rsqrt(spread + epsilon) * gain


def attend(packed, valid, head_count):
    length = packed.shape[0]
    model_width = packed.shape[1] // 3
    head_size = model_width // head_count
    scale_factor = 1.0 / jnp.sqrt(jnp.float32(head_size))
    queries = packed[:, :model_width].reshape(length, head_count, head_size)
    key_part = packed[:, model_width : 2 * model_width].reshape(length, head_count, head_size)
    value_part = packed[:, 2 * model_width :].reshape(length, head_count, head_size)
    scores = (
        jnp.einsum("qhd,khd->hqk", queries, key_part, preferred_element_type=jnp.float32)
        * scale_factor
    )
    scores = jnp.where(valid[None, None, :], scores, jnp.float32(-1e30))
    maxima = jnp.max(scores, axis=-1, keepdims=True)
    exponentials = jnp.where(valid[None, None, :], jnp.exp(scores - maxima), jnp.float32(0.0))
    totals = jnp.sum(exponentials, axis=-1, keepdims=True)
    probabilities = (exponentials / totals).astype(jnp.bfloat16)
    context = jnp.einsum(
        "hqk,khd->qhd", probabilities, value_part, preferred_element_type=jnp.float32
    )
    return context.reshape(length, model_width).astype(jnp.bfloat16)


def project(values, weight):
    flat = values.reshape(-1, values.shape[-1])
    return jnp.dot(flat, weight, preferred_element_type=jnp.float32).reshape(
        values.shape[:-1] + (weight.shape[1],)
    )


def body(
    table_cells,
    counts,
    train_count,
    norm_gain,
    feature_in,
    feature_out,
    sample_in,
    sample_out,
    hidden_up,
    hidden_down,
):
    row_local, feats_all, model_width = table_cells.shape
    feat_in_all, feat_out_all = (
        lax.all_gather(feature_in, "narrow", axis=0, tiled=True),
        lax.all_gather(feature_out, "narrow", axis=0, tiled=True),
    )
    feature_ids = jnp.arange(feats_all, dtype=jnp.int32)
    packed = project(table_cells, feat_in_all).astype(jnp.bfloat16)

    def feature_row(pair):
        return attend(pair[0], feature_ids < pair[1], HEADS)

    context = lax.map(feature_row, (packed, counts))
    update = project(context, feat_out_all)
    first = normalize(table_cells.astype(jnp.float32) + update, norm_gain[0]).astype(jnp.bfloat16)
    columns = lax.all_to_all(first, ("wide", "narrow"), split_axis=1, concat_axis=0, tiled=True)
    rows_all, feat_local = (columns.shape[0], columns.shape[1])
    samp_in_all, samp_out_all = (
        lax.all_gather(sample_in, "narrow", axis=0, tiled=True),
        lax.all_gather(sample_out, "narrow", axis=0, tiled=True),
    )
    by_feature = jnp.swapaxes(columns, 0, 1)
    valid = jnp.arange(rows_all, dtype=jnp.int32) < train_count[0]
    packed_samples = project(by_feature, samp_in_all).astype(jnp.bfloat16)
    sample_context = lax.map(lambda column: attend(column, valid, HEADS), packed_samples)
    sample_update = project(sample_context, samp_out_all)
    second = normalize(by_feature.astype(jnp.float32) + sample_update, norm_gain[1]).astype(
        jnp.bfloat16
    )
    up_all, down_all = (
        lax.all_gather(hidden_up, "narrow", axis=0, tiled=True),
        lax.all_gather(hidden_down, "narrow", axis=0, tiled=True),
    )
    hidden = jax.nn.gelu(project(second, up_all), approximate=False).astype(jnp.bfloat16)
    back = project(hidden, down_all)
    result = normalize(second.astype(jnp.float32) + back, norm_gain[2]).astype(jnp.bfloat16)
    result_rows = jnp.swapaxes(result, 0, 1)
    return lax.all_to_all(result_rows, ("wide", "narrow"), split_axis=0, concat_axis=1, tiled=True)


def solution(mesh):
    return jax.shard_map(
        body,
        mesh=mesh,
        in_specs=(
            P(("groups", "wide", "narrow"), None, None),
            P(("groups", "wide", "narrow")),
            P("groups"),
            P(),
            P("narrow", None),
            P("narrow", None),
            P("narrow", None),
            P("narrow", None),
            P("narrow", None),
            P("narrow", None),
        ),
        out_specs=P(("groups", "wide", "narrow"), None, None),
        check_vma=False,
    )
```

profile of v0, /device:TPU:0, one launch (start us, length us, event | category | flops | bytes accessed | tf_op | source)
XLA Modules:
  0.0 134.4 jit_solution(16577640377260590868)
XLA Ops:
  0.0 0.8 fusion.94
  0.8 15.2 %all_gather.19 = bf16[192,192]{1,0:T(8,128)(2,1)S(1)} all-gather(bf16[48,192]{1,0:T(8,128)(2,1)} %param.19), channel_id=1, replica_groups=mesh['groups'=1,'wide'=8,'narrow'=4] {'narrow'}, dimensions={0}, use_global_device_ids=true | all-gather | bytes 92160 | tf_op jit(solution)/shard_map/all_gather | solution.py:64
  16.0 14.4 %all_gather.18 = bf16[192,576]{1,0:T(8,128)(2,1)S(1)} all-gather(bf16[48,576]{1,0:T(8,128)(2,1)} %param.18), channel_id=1, replica_groups=mesh['groups'=1,'wide'=8,'narrow'=4] {'narrow'}, dimensions={0}, use_global_device_ids=true | all-gather | bytes 276480 | tf_op jit(solution)/shard_map/all_gather | solution.py:63
  30.5 1.3 convolution_convert_fusion.3
  31.8 9.3 %while.22 = (s32[]{:T(128)}, bf16[4,128,192]{1,2,0:T(8,128)(2,1)S(1)}, bf16[4,128,576]{1,2,0:T(8,128)(2,1)S(1)}, s32[4]{0:T(128)S(1)}, s32[]{:T(128)}) while((s32[]{:T(128)}, bf16[4,128,192]{1,2,0:T(8,128)(2,1)S(1)}, bf16[4,128,576]{1,2,0:T(8,128)(2,1)S(1)}, s32[4]{0:T(128)S(1)}, s32[]{:T(128)}) %tuple.61), condition=%wide.region_3.4_spmd.clone, body=%wide.region_0.3_spmd.clone.sunk | while | flops 19981440 | bytes 1776221 | solution.py:72
  31.8 0.7 dynamic_slice.20
  32.5 0.7 iota_compare_fusion.4
  34.1 0.7 dynamic_slice.20
  34.8 0.7 iota_compare_fusion.4
  36.5 0.7 dynamic_slice.20
  37.1 0.7 iota_compare_fusion.4
  38.8 0.7 dynamic_slice.20
  39.5 0.7 iota_compare_fusion.4
  41.6 0.9 copy.28
  42.5 5.3 %all-to-all-start = ((bf16[4,128,192]{2,0,1:T(4,128)(2,1)}), bf16[4,128,192]{2,0,1:T(4,128)(2,1)S(1)}, u32[]{:S(2)}, u32[]{:S(2)}) async-start(bf16[4,128,192]{2,0,1:T(4,128)(2,1)} %copy.28), calls=%async_computation | async-start | bytes 524288 | tf_op jit(solution)/shard_map/all_to_all | solution.py:75
  47.8 16.4 %all_gather.21 = bf16[192,192]{1,0:T(8,128)(2,1)S(1)} all-gather(bf16[48,192]{1,0:T(8,128)(2,1)S(1)} %copy-done.4), channel_id=1, replica_groups=mesh['groups'=1,'wide'=8,'narrow'=4] {'narrow'}, dimensions={0}, use_global_device_ids=true | all-gather | bytes 92160 | tf_op jit(solution)/shard_map/all_gather | solution.py:79
  64.3 13.8 %all_gather.20 = bf16[192,576]{1,0:T(8,128)(2,1)S(1)} all-gather(bf16[48,576]{1,0:T(8,128)(2,1)S(1)} %copy-done.3), channel_id=1, replica_groups=mesh['groups'=1,'wide'=8,'narrow'=4] {'narrow'}, dimensions={0}, use_global_device_ids=true | all-gather | bytes 276480 | tf_op jit(solution)/shard_map/all_gather | solution.py:78
  78.1 14.3 %all_gather.22 = bf16[192,768]{1,0:T(8,128)(2,1)S(1)} all-gather(bf16[48,768]{1,0:T(8,128)(2,1)S(1)} %copy-done.2), channel_id=1, replica_groups=mesh['groups'=1,'wide'=8,'narrow'=4] {'narrow'}, dimensions={0}, use_global_device_ids=true | all-gather | bytes 368640 | tf_op jit(solution)/shard_map/all_gather | solution.py:90
  92.3 14.2 %all_gather.23 = bf16[768,192]{1,0:T(8,128)(2,1)S(1)} all-gather(bf16[192,192]{1,0:T(8,128)(2,1)S(1)} %copy-done.1), channel_id=1, replica_groups=mesh['groups'=1,'wide'=8,'narrow'=4] {'narrow'}, dimensions={0}, use_global_device_ids=true | all-gather | bytes 368640 | tf_op jit(solution)/shard_map/all_gather | solution.py:91
  107.3 6.4 %while.23 = (s32[]{:T(128)}, bf16[4,128,192]{1,2,0:T(8,128)(2,1)S(1)}, bf16[4,128,576]{1,2,0:T(8,128)(2,1)S(1)}, s32[]{:T(128)}, s32[]{:T(128)}) while((s32[]{:T(128)}, bf16[4,128,192]{1,2,0:T(8,128)(2,1)S(1)}, bf16[4,128,576]{1,2,0:T(8,128)(2,1)S(1)}, s32[]{:T(128)}, s32[]{:T(128)}) %tuple.58), condition=%wide.region_9.10_spmd.clone, body=%wide.region_6.9_spmd.clone.sunk | while | flops 19981440 | bytes 1776209 | solution.py:84
  114.2 0.8 fusion.43
  115.0 3.8 %fusion.46 = (f32[4,128]{1,0:T(4,128)S(1)}, f32[4,128,192]{1,2,0:T(8,128)S(1)}) fusion(bf16[4,128,192]{1,2,0:T(8,128)(2,1)S(1)} %multiply_convert_fusion, bf16[768,192]{1,0:T(8,128)(2,1)S(1)} %all_gather.23, f32[4,128,768]{2,1,0:T(8,128)S(1)} %get-tuple-element.114, u8[128,768]{1,0:T(8,128)(4,1)S(1)} %get-tuple-element.78, ...), kind=kOutput, calls=%fused_computation.80 | convolution fusion | flops 178814464 | bytes 2656256 | tf_op jit(solution)/shard_map/dot_general | solution.py:44
  119.2 14.2 %all_to_all.36 = bf16[128,4,192]{2,1,0:T(4,128)(2,1)S(1)} all-to-all(bf16[128,4,192]{2,1,0:T(4,128)(2,1)S(1)} %copy.33), channel_id=1, replica_groups=mesh['groups'=1,'wide'=8,'narrow'=4] {'wide','narrow'}, dimensions={0} | all-to-all | bytes 393216 | tf_op jit(solution)/shard_map/all_to_all | solution.py:97
  133.6 0.9 copy.35
  (86 shorter events, 12.1 us)
Async XLA Ops:
  0.0 31.8 %copy-start.5 = (s32[4]{0:T(128)S(1)}, s32[4]{0:T(128)}, u32[]{:S(2)}) copy-start(s32[4]{0:T(128)} %param.15) | copy-start | bytes 52
  31.8 9.3 %copy-start = (bf16[4,128,192]{1,2,0:T(8,128)(2,1)S(1)}, bf16[4,128,192]{1,2,0:T(8,128)(2,1)}, u32[]{:S(2)}) copy-start(bf16[4,128,192]{1,2,0:T(8,128)(2,1)} %param.14) | copy-start | bytes 589828
  41.1 6.7 %copy-start.4 = (bf16[48,192]{1,0:T(8,128)(2,1)S(1)}, bf16[48,192]{1,0:T(8,128)(2,1)}, u32[]{:S(2)}) copy-start(bf16[48,192]{1,0:T(8,128)(2,1)} %param.21) | copy-start | bytes 55300
  41.1 23.2 %copy-start.3 = (bf16[48,576]{1,0:T(8,128)(2,1)S(1)}, bf16[48,576]{1,0:T(8,128)(2,1)}, u32[]{:S(2)}) copy-start(bf16[48,576]{1,0:T(8,128)(2,1)} %param.20) | copy-start | bytes 165892
  41.1 36.9 %copy-start.2 = (bf16[48,768]{1,0:T(8,128)(2,1)S(1)}, bf16[48,768]{1,0:T(8,128)(2,1)}, u32[]{:S(2)}) copy-start(bf16[48,768]{1,0:T(8,128)(2,1)} %param.22) | copy-start | bytes 221188
  41.4 50.9 %copy-start.1 = (bf16[192,192]{1,0:T(8,128)(2,1)S(1)}, bf16[192,192]{1,0:T(8,128)(2,1)}, u32[]{:S(2)}) copy-start(bf16[192,192]{1,0:T(8,128)(2,1)} %param.23) | copy-start | bytes 221188
  42.5 64.1 %all-to-all-start = ((bf16[4,128,192]{2,0,1:T(4,128)(2,1)}), bf16[4,128,192]{2,0,1:T(4,128)(2,1)S(1)}, u32[]{:S(2)}, u32[]{:S(2)}) async-start(bf16[4,128,192]{2,0,1:T(4,128)(2,1)} %copy.28), calls=%async_computation | async-start | bytes 524288 | tf_op jit(solution)/shard_map/all_to_all | solution.py:75
where the time goes:
time: 135 us; the launch traced here: 134 us
  blocking collectives  103 us (76%)
  matrix products  13.6 us (10%)
  local copies, waits for them, and re-layouts  6.32 us (5%)
  other arithmetic  5.99 us (4%)
  starting transfers between devices  5.33 us (4%)
    all_gather x1, blocking collectives, body(): lax.all_gather(sample_out, 'narrow', axis=0, tiled=True)  16.4 us
    all_gather x1, blocking collectives, body(): lax.all_gather(feature_out, 'narrow', axis=0, tiled=True)  15.2 us
    all_gather x1, blocking collectives, body(): lax.all_gather(feature_in, 'narrow', axis=0, tiled=True)  14.4 us
    all_gather x1, blocking collectives, body(): lax.all_gather(hidden_up, 'narrow', axis=0, tiled=True)  14.3 us
    all_to_all x1, blocking collectives, body(): lax.all_to_all(result_rows, ('wide', 'narrow'), split_axis=0, concat_axis...  14.2 us
    all_gather x1, blocking collectives, body(): lax.all_gather(hidden_down, 'narrow', axis=0, tiled=True)  14.2 us
    all_gather x1, blocking collectives, body(): lax.all_gather(sample_in, 'narrow', axis=0, tiled=True)  13.8 us
    dot_general x6, matrix products, project(): jnp.dot(flat, weight, preferred_element_type=jnp.float32)  6.72 us
  transfers between devices with their start and end apart: 1, of which 0 were waited for; matrix products, arithmetic and copies ran while one was open for 0% of the time, Pallas kernels for 0%

commit v1 on v0

v1 whole, which is shorter than its diff:
```python
import functools
import math

import jax
import jax.numpy as jnp
from jax import lax
from jax.experimental import pallas as pl
from jax.experimental.pallas import tpu as pltpu
from jax.sharding import PartitionSpec as P

HEADS = 6
EPSILON = 1e-05
MESH = pl.DeviceIdType.MESH
F32 = jnp.float32
BF16 = jnp.bfloat16


def normalize(values, gain):
    average = jnp.mean(values, axis=-1, keepdims=True)
    centered = values - average
    spread = jnp.mean(centered * centered, axis=-1, keepdims=True)
    return centered * lax.rsqrt(spread + EPSILON) * gain


def matmul(a, b):
    return jnp.dot(a, b, preferred_element_type=F32)


def gathered(ref, half):
    parts, _, rows, columns = ref.shape
    if rows % 16 == 0:
        return ref[:, half].reshape(parts * rows, columns)
    pieces = [ref[i, half].astype(F32) for i in range(parts)]
    return jnp.concatenate(pieces, axis=0).astype(BF16)


def reorder(x, source, chunk=512):
    count = x.shape[0]
    chunk = min(chunk, count)
    pieces = []
    for start in range(0, count, chunk):
        to = lax.broadcasted_iota(jnp.int32, (chunk, 1), 0) + start
        column = lax.broadcasted_iota(jnp.int32, (chunk, count), 1)
        pick = jnp.where(column == source(to), 1.0, 0.0).astype(BF16)
        pieces.append(matmul(pick, x).astype(BF16))
    return pieces[0] if len(pieces) == 1 else jnp.concatenate(pieces, axis=0)


def attend(q, k, v, bias):
    length, width = q.shape
    head_size = width // HEADS
    factor = math.log2(math.e) / math.sqrt(head_size)
    head_of = lax.broadcasted_iota(jnp.int32, (length, width), 1) // head_size
    zero = jnp.zeros_like(k)
    masks = [head_of == h for h in range(HEADS)]
    keys = jnp.concatenate([jnp.where(m, k, zero) for m in masks], axis=0)
    values = jnp.concatenate([jnp.where(m, v, zero) for m in masks], axis=0)
    ones = jnp.concatenate([jnp.where(m, 1.0, 0.0).astype(BF16) for m in masks], axis=0)
    scores = lax.dot_general(q, keys, (((1,), (1,)), ((), ())), preferred_element_type=F32)
    powers = []
    for h in range(HEADS):
        s = scores[:, h * length : (h + 1) * length] * factor + bias
        powers.append(jnp.exp2(s - jnp.max(s, axis=-1, keepdims=True)).astype(BF16))
    weight = jnp.concatenate(powers, axis=1)
    return (matmul(weight, values) / matmul(weight, ones)).astype(BF16)


def attention_block(x, w_ref, qkv_ref, ctx_ref, length, bias_of, gain):
    width = x.shape[1]
    left, right = gathered(w_ref, 0), gathered(w_ref, 1)
    qk = matmul(x, left).astype(BF16)
    qkv_ref[0] = qk[:, :width]
    qkv_ref[1] = qk[:, width:]
    qkv_ref[2] = matmul(x, right[:, :width]).astype(BF16)

    def one(i):
        rows = pl.ds(pl.multiple_of(i * length, length), length)
        ctx_ref[rows, :] = attend(
            qkv_ref[0, rows, :], qkv_ref[1, rows, :], qkv_ref[2, rows, :], bias_of(i)
        )

    count = x.shape[0] // length
    if length <= 128:
        for i in range(count):
            one(i)
    else:
        pl.loop(0, count)(one)
    update = matmul(ctx_ref[...], right[:, width:])
    return normalize(x.astype(F32) + update, gain).astype(BF16)


def kernel(
    sizes,
    counts_ref,
    train_ref,
    cells_ref,
    gain_ref,
    fi_ref,
    fo_ref,
    si_ref,
    so_ref,
    hu_ref,
    hd_ref,
    out_ref,
    wf,
    ws,
    wu,
    wd,
    qkv,
    ctx,
    send1,
    recv1,
    send2,
    recv2,
    sa,
    ra,
    sb,
    rb,
    cell_sems,
):
    wide, narrow = sizes
    total = wide * narrow
    g = lax.axis_index("groups")
    w = lax.axis_index("wide")
    n = lax.axis_index("narrow")
    me = w * narrow + n
    core = lax.rem(w, 2)
    mate = w + 1 - 2 * core
    rows, feats, width = cells_ref.shape
    local = feats // total
    block = rows * local
    all_rows = rows * total
    cells = rows * feats

    def device(d):
        return (g, d // narrow, lax.rem(d, narrow))

    barrier = pltpu.get_barrier_semaphore()

    @pl.loop(1, total)
    def _(step):
        pl.semaphore_signal(
            barrier, inc=1, device_id=device(lax.rem(me + step, total)), device_id_type=MESH
        )

    half = 2 * width
    wf[n, 0] = fi_ref[:, :half]
    wf[n, 1] = jnp.concatenate([fi_ref[:, half:], fo_ref[...]], axis=1)
    ws[n, 0] = si_ref[:, :half]
    ws[n, 1] = jnp.concatenate([si_ref[:, half:], so_ref[...]], axis=1)
    wu[n, 0] = hu_ref[:, :half]
    wu[n, 1] = hu_ref[:, half:]
    down = hd_ref.shape[0] // 2
    wd[n, 0] = hd_ref[:down]
    wd[n, 1] = hd_ref[down:]
    pl.semaphore_wait(barrier, total - 1)

    weights = (wf, ws, wu, wd)

    def along(group, step):
        ref = weights[group]
        return pltpu.make_async_remote_copy(
            src_ref=ref.at[n, core],
            dst_ref=ref.at[n, core],
            send_sem=sa.at[group, step],
            recv_sem=ra.at[group, step],
            device_id=(g, w, lax.rem(n + step, narrow)),
            device_id_type=MESH,
        )

    def across(group, step):
        ref = weights[group]
        owner = lax.rem(n - step + narrow, narrow)
        return pltpu.make_async_remote_copy(
            src_ref=ref.at[owner, core],
            dst_ref=ref.at[owner, core],
            send_sem=sb.at[group, step],
            recv_sem=rb.at[group, step],
            device_id=(g, mate, n),
            device_id_type=MESH,
        )

    steps = range(1, narrow)
    for group in range(4):
        for step in steps:
            along(group, step).start()

    def forward(group):
        for step in steps:
            along(group, step).wait_recv()
            across(group, step).start()

    def arrive(group):
        for step in steps:
            across(group, step).wait_recv()

    def exchange(send, recv, index):
        recv[me] = send[me]

        @pl.loop(1, total)
        def _(step):
            d = lax.rem(me + step, total)
            pltpu.make_async_remote_copy(
                src_ref=send.at[d],
                dst_ref=recv.at[me],
                send_sem=cell_sems.at[index],
                recv_sem=cell_sems.at[index + 1],
                device_id=device(d),
                device_id_type=MESH,
            ).start()

    def exchanged(send, recv, index):
        for ref, sem in ((recv, index + 1), (send, index)):
            whole = ref.at[pl.ds(0, total - 1)]
            pltpu.make_async_copy(whole, whole, cell_sems.at[sem]).wait()

    forward(0)
    arrive(0)
    x = cells_ref[...].reshape(cells, width)
    keys = lax.broadcasted_iota(jnp.int32, (1, feats), 1)

    def row_bias(i):
        return jnp.where(keys < counts_ref[i], 0.0, -1e30)

    first = attention_block(x, wf, qkv, ctx, feats, row_bias, gain_ref[0:1, :])

    def to_send(i):
        d, j, r = i // block, (i % block) // rows, i % rows
        return r * feats + d * local + j

    send1[...] = reorder(first, to_send).reshape(total, block, width)
    exchange(send1, recv1, 0)
    for group in (1, 2, 3):
        forward(group)
    arrive(1)
    exchanged(send1, recv1, 0)

    def to_column(i):
        j, s, r = i // all_rows, (i % all_rows) // rows, i % rows
        return s * block + j * rows + r

    y = reorder(recv1[...].reshape(cells, width), to_column)
    samples = lax.broadcasted_iota(jnp.int32, (1, all_rows), 1)
    sample_bias = jnp.where(samples < train_ref[0], 0.0, -1e30)
    second = attention_block(y, ws, qkv, ctx, all_rows, lambda i: sample_bias, gain_ref[1:2, :])

    arrive(2)
    arrive(3)
    ctx[...] = second
    tile = min(512, cells)
    up = [gathered(wu, c) for c in range(2)]
    parts, _, depth, _ = wd.shape
    hidden_width = up[0].shape[1]

    def feed(i):
        at = pl.ds(pl.multiple_of(i * tile, tile), tile)
        values = ctx[at, :]
        halves = []
        for c in range(2):
            h = matmul(values, up[c])
            halves.append((0.5 * h * (1.0 + lax.erf(h * (2.0**-0.5)))).astype(BF16))
        hidden = jnp.concatenate(halves, axis=1)
        back = matmul(hidden, wd[...].reshape(2 * hidden_width, width))
        ctx[at, :] = normalize(values.astype(F32) + back, gain_ref[2:3, :]).astype(BF16)

    if cells == tile:
        feed(0)
    else:
        pl.loop(0, cells // tile)(feed)

    def to_return(i):
        s, j, r = i // block, (i % block) // rows, i % rows
        return j * all_rows + s * rows + r

    send2[...] = reorder(ctx[...], to_return).reshape(total, block, width)
    exchange(send2, recv2, 2)
    for group in range(4):
        for step in steps:
            along(group, step).wait_send()
            across(group, step).wait_send()
    exchanged(send2, recv2, 2)

    def to_row(i):
        r, d, j = i // feats, (i % feats) // local, i % local
        return d * block + j * rows + r

    out_ref[...] = reorder(recv2[...].reshape(cells, width), to_row).reshape(rows, feats, width)


def body(sizes, cells, counts, train, gain, fi, fo, si, so, hu, hd):
    wide, narrow = sizes
    total = wide * narrow
    rows, feats, width = cells.shape
    block = rows * (feats // total)
    shard = fi.shape[0]
    vmem = pl.BlockSpec(memory_space=pltpu.VMEM)
    smem = pl.BlockSpec(memory_space=pltpu.SMEM)
    blocks = pltpu.VMEM((total, block, width), BF16)
    sems = pltpu.SemaphoreType.DMA((4, narrow))
    weight = pltpu.VMEM((narrow, 2, shard, 2 * width), BF16)
    return pl.pallas_call(
        functools.partial(kernel, sizes),
        out_shape=jax.ShapeDtypeStruct(cells.shape, BF16),
        in_specs=[smem, smem] + [vmem] * 8,
        out_specs=vmem,
        scratch_shapes=[
            weight,
            weight,
            weight,
            pltpu.VMEM((narrow, 2, hd.shape[0] // 2, width), BF16),
            pltpu.VMEM((3, rows * feats, width), BF16),
            pltpu.VMEM((rows * feats, width), BF16),
            blocks,
            blocks,
            blocks,
            blocks,
            sems,
            sems,
            sems,
            sems,
            pltpu.SemaphoreType.DMA((4,)),
        ],
        compiler_params=pltpu.CompilerParams(
            collective_id=0, has_side_effects=True, vmem_limit_bytes=56 << 20
        ),
    )(counts, train, cells, gain, fi, fo, si, so, hu, hd)


def solution(mesh):
    sizes = (mesh.shape["wide"], mesh.shape["narrow"])
    return jax.shard_map(
        functools.partial(body, sizes),
        mesh=mesh,
        in_specs=(
            P(("groups", "wide", "narrow"), None, None),
            P(("groups", "wide", "narrow")),
            P("groups"),
            P(),
            P("narrow", None),
            P("narrow", None),
            P("narrow", None),
            P("narrow", None),
            P("narrow", None),
            P("narrow", None),
        ),
        out_specs=P(("groups", "wide", "narrow"), None, None),
        check_vma=False,
    )
```

time: 135 us -> 48 us (0.36)
  blocking collectives: 103 us -> 0 us
  Pallas kernels: 0 us -> 43.6 us
  matrix products: 13.6 us -> 0 us
  other arithmetic: 5.99 us -> 0 us
  starting transfers between devices: 5.33 us -> 0 us
  local copies, waits for them, and re-layouts: 6.32 us -> 3.52 us
    all_gather x6 -> x0, blocking collectives: 88.3 us -> none  [the longest x1 16.4 us: body(): lax.all_gather(sample_out, 'narrow', axis=0, tiled=True)]
    pallas_call x0 -> x1, Pallas kernels: none -> 43.6 us  [body(): pl.pallas_call(functools.partial(kernel, sizes), out_shape=jax.ShapeDtype...]
    all_to_all x1 -> x0, blocking collectives: 14.2 us -> none  [body(): lax.all_to_all(result_rows, ('wide', 'narrow'), split_axis=0, concat_axis...]
    dot_general x22 -> x0, matrix products: 10.7 us -> none  [the longest x6 6.72 us: project(): jnp.dot(flat, weight, preferred_element_type=jnp.float32)]
    lt x8 -> x0, other arithmetic: 5.38 us -> none  [the longest x4 2.77 us: feature_row(): return attend(pair[0], feature_ids < pair[1], HEADS)]
    all_to_all x1 -> x0, starting transfers between devices: 5.33 us -> none  [body(): lax.all_to_all(first, ('wide', 'narrow'), split_axis=1, concat_axis=0, ti...]
    sub x8 -> x0, matrix products: 2.84 us -> none  [attend(): scores - maxima]
    dynamic_slice x4 -> x0, local copies, waits for them, and re-layouts: 2.67 us -> none  [body(): context = lax.map(feature_row, (packed, counts))]
  transfers between devices with their start and end apart: 1 -> 0, of which waited for: 0 -> 0; matrix products, arithmetic and copies ran while one was open for 0% -> 0% of each run, Pallas kernels for 0% -> 0%
where the time goes in v1:
time: 48 us; the launch traced here: 47.8 us
  Pallas kernels  43.6 us (91%)
  local copies, waits for them, and re-layouts  3.52 us (7%)
  between operations  0.66 us (1%)
    pallas_call x1, Pallas kernels, body(): pl.pallas_call(functools.partial(kernel, sizes), out_shape=jax.ShapeDtype...  43.6 us
    pallas_call x1, local copies, waits for them, and re-layouts, body(): pl.pallas_call(functools.partial(kernel, sizes), out_shape=jax.ShapeDtype...  1.77 us
    unnamed x1, local copies, waits for them, and re-layouts  1.76 us

profile of v1, /device:TPU:0, one launch (start us, length us, event | category | flops | bytes accessed | tf_op | source)
XLA Modules:
  0.0 47.8 jit_solution(14322660898189916235)
XLA Ops:
  0.7 1.8 %copy.11.cells_ref = bf16[4,128,192]{2,1,0:T(8,128)(2,1)} copy(bf16[4,128,192]{1,2,0:T(8,128)(2,1)} %param.10) | data formatting | bytes 393216 | tf_op args[0]
  2.4 43.6 %shard_map.100 = bf16[4,128,192]{2,1,0:T(8,128)(2,1)} custom-call(s32[4]{0:T(128)} %counts_ref.1, s32[1]{0:T(128)S(6)} %copy.13.train_ref, bf16[4,128,192]{2,1,0:T(8,128)(2,1)} %copy.11.cells_ref, f32[3,192]{1,0:T(4,128)} %gain_ref.1, bf16[48,576]{1,0:T(8,128)(2,1)} %fi_ref.1, bf16[48,192]{1,0:T(8,128)(2,1)} %fo_ref.1, bf16[48,576]{1,0:T(8,128)(2,1)} %si_ref.1, ...), custom_call_target="tpu_custom_call" | custom-call | tf_op jit(solution)/shard_map/pallas_call | solution.py:301
  46.0 1.8 %copy.12 = bf16[4,128,192]{1,2,0:T(8,128)(2,1)} copy(bf16[4,128,192]{2,1,0:T(8,128)(2,1)} %shard_map.100) | data formatting | bytes 393216 | tf_op jit(solution)/shard_map/pallas_call | solution.py:301

commit v2 on v1

--- a/solution.py
+++ b/solution.py
@@ -26,23 +26,35 @@
     return jnp.dot(a, b, preferred_element_type=F32)
 
 
-def gathered(ref, half):
+def gathered(ref, part):
     parts, _, rows, columns = ref.shape
     if rows % 16 == 0:
-        return ref[:, half].reshape(parts * rows, columns)
-    pieces = [ref[i, half].astype(F32) for i in range(parts)]
+        return ref[:, part].reshape(parts * rows, columns)
+    pieces = [ref[i, part].astype(F32) for i in range(parts)]
     return jnp.concatenate(pieces, axis=0).astype(BF16)
 
 
-def reorder(x, source, chunk=512):
-    count = x.shape[0]
+def gathered_down(ref, width):
+    pieces = []
+    for owner in range(ref.shape[0]):
+        for part in (2, 3):
+            both = ref[owner, part].astype(F32)
+            pieces += [both[:, :width], both[:, width:]]
+    return jnp.concatenate(pieces, axis=0).astype(BF16)
+
+
+def one_hot(count, depth, start, source):
+    to = lax.broadcasted_iota(jnp.int32, (count, 1), 0) + start
+    column = lax.broadcasted_iota(jnp.int32, (count, depth), 1)
+    return jnp.where(column == source(to), 1.0, 0.0).astype(BF16)
+
+
+def reorder(x, count, source, chunk=512):
     chunk = min(chunk, count)
-    pieces = []
-    for start in range(0, count, chunk):
-        to = lax.broadcasted_iota(jnp.int32, (chunk, 1), 0) + start
-        column = lax.broadcasted_iota(jnp.int32, (chunk, count), 1)
-        pick = jnp.where(column == source(to), 1.0, 0.0).astype(BF16)
-        pieces.append(matmul(pick, x).astype(BF16))
+    pieces = [
+        matmul(one_hot(chunk, x.shape[0], start, source), x)
+        for start in range(0, count, chunk)
+    ]
     return pieces[0] if len(pieces) == 1 else jnp.concatenate(pieces, axis=0)
 
 
@@ -65,9 +77,9 @@
     return (matmul(weight, values) / matmul(weight, ones)).astype(BF16)
 
 
-def attention_block(x, w_ref, qkv_ref, ctx_ref, length, bias_of, gain):
+def attention_block(x, w_ref, part, qkv_ref, ctx_ref, length, bias_of, gain):
     width = x.shape[1]
-    left, right = gathered(w_ref, 0), gathered(w_ref, 1)
+    left, right = gathered(w_ref, part), gathered(w_ref, part + 1)
     qk = matmul(x, left).astype(BF16)
     qkv_ref[0] = qk[:, :width]
     qkv_ref[1] = qk[:, width:]
@@ -93,19 +105,24 @@
     sizes,
     counts_ref,
     train_ref,
+    gain_ref,
+    cells_hbm,
+    fi_hbm,
+    fo_hbm,
+    si_hbm,
+    so_hbm,
+    hu_hbm,
+    hd_hbm,
+    out_ref,
     cells_ref,
-    gain_ref,
     fi_ref,
     fo_ref,
     si_ref,
     so_ref,
     hu_ref,
     hd_ref,
-    out_ref,
-    wf,
-    ws,
-    wu,
-    wd,
+    wa,
+    wb,
     qkv,
     ctx,
     send1,
@@ -114,9 +131,12 @@
     recv2,
     sa,
     ra,
+    sx,
+    rx,
     sb,
     rb,
     cell_sems,
+    load_sems,
 ):
     wide, narrow = sizes
     total = wide * narrow
@@ -126,6 +146,10 @@
     me = w * narrow + n
     core = lax.rem(w, 2)
     mate = w + 1 - 2 * core
+    part = lax.rem(w, 4)
+    side = part // 2
+    near = w + 2 - 4 * side
+    far_part = part + 2 - 4 * side
     rows, feats, width = cells_ref.shape
     local = feats // total
     block = rows * local
@@ -143,56 +167,99 @@
             barrier, inc=1, device_id=device(lax.rem(me + step, total)), device_id_type=MESH
         )
 
+    loads = [
+        pltpu.make_async_copy(src, dst, load_sems.at[i])
+        for i, (src, dst) in enumerate(
+            (
+                (fi_hbm, fi_ref),
+                (fo_hbm, fo_ref),
+                (si_hbm, si_ref),
+                (so_hbm, so_ref),
+                (hu_hbm, hu_ref),
+                (hd_hbm, hd_ref),
+                (cells_hbm, cells_ref),
+            )
+        )
+    ]
+    for load in loads:
+        load.start()
     half = 2 * width
-    wf[n, 0] = fi_ref[:, :half]
-    wf[n, 1] = jnp.concatenate([fi_ref[:, half:], fo_ref[...]], axis=1)
-    ws[n, 0] = si_ref[:, :half]
-    ws[n, 1] = jnp.concatenate([si_ref[:, half:], so_ref[...]], axis=1)
-    wu[n, 0] = hu_ref[:, :half]
-    wu[n, 1] = hu_ref[:, half:]
-    down = hd_ref.shape[0] // 2
-    wd[n, 0] = hd_ref[:down]
-    wd[n, 1] = hd_ref[down:]
+    shard = fi_ref.shape[0]
+    for load in loads[:4]:
+        load.wait()
+    wa[n, 0] = fi_ref[:, :half]
+    wa[n, 1] = jnp.concatenate([fi_ref[:, half:], fo_ref[...]], axis=1)
+    wa[n, 2] = si_ref[:, :half]
+    wa[n, 3] = jnp.concatenate([si_ref[:, half:], so_ref[...]], axis=1)
+    for load in loads[4:]:
+        load.wait()
+    wb[n, 0] = hu_ref[:, :half]
+    wb[n, 1] = hu_ref[:, half:]
+    down = hd_ref[...].astype(F32)
+    for i in range(2):
+        top = down[2 * i * shard : (2 * i + 1) * shard]
+        low = down[(2 * i + 1) * shard : (2 * i + 2) * shard]
+        wb[n, 2 + i] = jnp.concatenate([top, low], axis=1).astype(BF16)
     pl.semaphore_wait(barrier, total - 1)
 
-    weights = (wf, ws, wu, wd)
+    weights = (wa, wb)
 
     def along(group, step):
         ref = weights[group]
         return pltpu.make_async_remote_copy(
-            src_ref=ref.at[n, core],
-            dst_ref=ref.at[n, core],
+            src_ref=ref.at[n, part],
+            dst_ref=ref.at[n, part],
             send_sem=sa.at[group, step],
             recv_sem=ra.at[group, step],
             device_id=(g, w, lax.rem(n + step, narrow)),
             device_id_type=MESH,
         )
 
-    def across(group, step):
+    def beside(group, step):
         ref = weights[group]
         owner = lax.rem(n - step + narrow, narrow)
         return pltpu.make_async_remote_copy(
-            src_ref=ref.at[owner, core],
-            dst_ref=ref.at[owner, core],
-            send_sem=sb.at[group, step],
-            recv_sem=rb.at[group, step],
+            src_ref=ref.at[owner, part],
+            dst_ref=ref.at[owner, part],
+            send_sem=sx.at[group, step],
+            recv_sem=rx.at[group, step],
+            device_id=(g, near, n),
+            device_id_type=MESH,
+        )
+
+    def across(group, far, step):
+        ref = weights[group]
+        owner = lax.rem(n - step + narrow, narrow)
+        which = far_part if far else part
+        return pltpu.make_async_remote_copy(
+            src_ref=ref.at[owner, which],
+            dst_ref=ref.at[owner, which],
+            send_sem=sb.at[group, far, step],
+            recv_sem=rb.at[group, far, step],
             device_id=(g, mate, n),
             device_id_type=MESH,
         )
 
     steps = range(1, narrow)
-    for group in range(4):
+    for group in range(2):
         for step in steps:
             along(group, step).start()
 
     def forward(group):
         for step in steps:
             along(group, step).wait_recv()
-            across(group, step).start()
+            beside(group, step).start()
+            across(group, 0, step).start()
+
+    def forward_far(group):
+        for step in steps:
+            beside(group, step).wait_recv()
+            across(group, 1, step).start()
 
     def arrive(group):
         for step in steps:
-            across(group, step).wait_recv()
+            across(group, 0, step).wait_recv()
+            across(group, 1, step).wait_recv()
 
     def exchange(send, recv, index):
         recv[me] = send[me]
@@ -214,7 +281,16 @@
             whole = ref.at[pl.ds(0, total - 1)]
             pltpu.make_async_copy(whole, whole, cell_sems.at[sem]).wait()
 
+    def packed(first, second):
+        both = jnp.concatenate([first, second], axis=1)
+        return both.reshape(total, block // 2, 2 * width).astype(BF16)
+
+    def unpacked(ref):
+        both = ref[...].astype(F32).reshape(cells // 2, 2 * width).astype(BF16)
+        return both[:, :width], both[:, width:]
+
     forward(0)
+    forward_far(0)
     arrive(0)
     x = cells_ref[...].reshape(cells, width)
     keys = lax.broadcasted_iota(jnp.int32, (1, feats), 1)
@@ -222,35 +298,41 @@
     def row_bias(i):
         return jnp.where(keys < counts_ref[i], 0.0, -1e30)
 
-    first = attention_block(x, wf, qkv, ctx, feats, row_bias, gain_ref[0:1, :])
+    first = attention_block(x, wa, 0, qkv, ctx, feats, row_bias, gain_ref[0:1, :])
+
+    part_rows = block // 2
+    part_cells = cells // 2
 
     def to_send(i):
-        d, j, r = i // block, (i % block) // rows, i % rows
-        return r * feats + d * local + j
-
-    send1[...] = reorder(first, to_send).reshape(total, block, width)
+        h, k = i // part_cells, i % part_cells
+        d, j, r = k // part_rows, (k % part_rows) // rows, k % rows
+        return r * feats + d * local + h * (local // 2) + j
+
+    picked = reorder(first, cells, to_send)
+    send1[...] = packed(picked[:part_cells], picked[part_cells:])
     exchange(send1, recv1, 0)
-    for group in (1, 2, 3):
-        forward(group)
-    arrive(1)
+    forward(1)
+    forward_far(1)
     exchanged(send1, recv1, 0)
 
     def to_column(i):
         j, s, r = i // all_rows, (i % all_rows) // rows, i % rows
-        return s * block + j * rows + r
-
-    y = reorder(recv1[...].reshape(cells, width), to_column)
+        return s * part_rows + j * rows + r
+
+    y = jnp.concatenate(
+        [reorder(v, part_cells, to_column).astype(BF16) for v in unpacked(recv1)], axis=0
+    )
     samples = lax.broadcasted_iota(jnp.int32, (1, all_rows), 1)
     sample_bias = jnp.where(samples < train_ref[0], 0.0, -1e30)
-    second = attention_block(y, ws, qkv, ctx, all_rows, lambda i: sample_bias, gain_ref[1:2, :])
-
-    arrive(2)
-    arrive(3)
+    second = attention_block(
+        y, wa, 2, qkv, ctx, all_rows, lambda i: sample_bias, gain_ref[1:2, :]
+    )
+
+    arrive(1)
     ctx[...] = second
     tile = min(512, cells)
-    up = [gathered(wu, c) for c in range(2)]
-    parts, _, depth, _ = wd.shape
-    hidden_width = up[0].shape[1]
+    up = [gathered(wb, c) for c in range(2)]
+    low = gathered_down(wb, width)
 
     def feed(i):
         at = pl.ds(pl.multiple_of(i * tile, tile), tile)
@@ -259,8 +341,7 @@
         for c in range(2):
             h = matmul(values, up[c])
             halves.append((0.5 * h * (1.0 + lax.erf(h * (2.0**-0.5)))).astype(BF16))
-        hidden = jnp.concatenate(halves, axis=1)
-        back = matmul(hidden, wd[...].reshape(2 * hidden_width, width))
+        back = matmul(jnp.concatenate(halves, axis=1), low)
         ctx[at, :] = normalize(values.astype(F32) + back, gain_ref[2:3, :]).astype(BF16)
 
     if cells == tile:
@@ -269,22 +350,29 @@
         pl.loop(0, cells // tile)(feed)
 
     def to_return(i):
-        s, j, r = i // block, (i % block) // rows, i % rows
+        s, j, r = i // part_rows, (i % part_rows) // rows, i % rows
         return j * all_rows + s * rows + r
 
-    send2[...] = reorder(ctx[...], to_return).reshape(total, block, width)
+    send2[...] = packed(
+        reorder(ctx[:part_cells, :], part_cells, to_return),
+        reorder(ctx[part_cells:, :], part_cells, to_return),
+    )
     exchange(send2, recv2, 2)
-    for group in range(4):
+    for group in range(2):
         for step in steps:
             along(group, step).wait_send()
-            across(group, step).wait_send()
+            beside(group, step).wait_send()
+            across(group, 0, step).wait_send()
+            across(group, 1, step).wait_send()
     exchanged(send2, recv2, 2)
 
     def to_row(i):
         r, d, j = i // feats, (i % feats) // local, i % local
-        return d * block + j * rows + r
-
-    out_ref[...] = reorder(recv2[...].reshape(cells, width), to_row).reshape(rows, feats, width)
+        h = j // (local // 2)
+        return h * part_cells + d * part_rows + (j % (local // 2)) * rows + r
+
+    landed = jnp.concatenate(unpacked(recv2), axis=0)
+    out_ref[...] = reorder(landed, cells, to_row).astype(BF16).reshape(rows, feats, width)
 
 
 def body(sizes, cells, counts, train, gain, fi, fo, si, so, hu, hd):
@@ -295,19 +383,19 @@
     shard = fi.shape[0]
     vmem = pl.BlockSpec(memory_space=pltpu.VMEM)
     smem = pl.BlockSpec(memory_space=pltpu.SMEM)
-    blocks = pltpu.VMEM((total, block, width), BF16)
-    sems = pltpu.SemaphoreType.DMA((4, narrow))
-    weight = pltpu.VMEM((narrow, 2, shard, 2 * width), BF16)
+    blocks = pltpu.VMEM((total, block // 2, 2 * width), BF16)
+    sems = pltpu.SemaphoreType.DMA((2, narrow))
+    far_sems = pltpu.SemaphoreType.DMA((2, 2, narrow))
+    weight = pltpu.VMEM((narrow, 4, shard, 2 * width), BF16)
     return pl.pallas_call(
         functools.partial(kernel, sizes),
         out_shape=jax.ShapeDtypeStruct(cells.shape, BF16),
-        in_specs=[smem, smem] + [vmem] * 8,
+        in_specs=[smem, smem, vmem] + [pl.BlockSpec(memory_space=pl.ANY)] * 7,
         out_specs=vmem,
         scratch_shapes=[
+            *[pltpu.VMEM(a.shape, BF16) for a in (cells, fi, fo, si, so, hu, hd)],
             weight,
             weight,
-            weight,
-            pltpu.VMEM((narrow, 2, hd.shape[0] // 2, width), BF16),
             pltpu.VMEM((3, rows * feats, width), BF16),
             pltpu.VMEM((rows * feats, width), BF16),
             blocks,
@@ -318,12 +406,15 @@
             sems,
             sems,
             sems,
+            far_sems,
+            far_sems,
             pltpu.SemaphoreType.DMA((4,)),
+            pltpu.SemaphoreType.DMA((7,)),
         ],
         compiler_params=pltpu.CompilerParams(
             collective_id=0, has_side_effects=True, vmem_limit_bytes=56 << 20
         ),
-    )(counts, train, cells, gain, fi, fo, si, so, hu, hd)
+    )(counts, train, gain, cells, fi, fo, si, so, hu, hd)
 
 
 def solution(mesh):

time: 48 us -> 43.5 us (0.906)
  Pallas kernels: 43.6 us -> 39.1 us
    pallas_call x1, Pallas kernels: 43.6 us -> 39.1 us  [body(): pl.pallas_call(functools.partial(kernel, sizes), out_shape=jax.ShapeDtype...]
where the time goes in v2:
time: 43.5 us; the launch traced here: 43.2 us
  Pallas kernels  39.1 us (90%)
  local copies, waits for them, and re-layouts  3.52 us (8%)
  between operations  0.66 us (2%)
    pallas_call x1, Pallas kernels, body(): pl.pallas_call(functools.partial(kernel, sizes), out_shape=jax.ShapeDtype...  39.1 us
    pallas_call x1, local copies, waits for them, and re-layouts, body(): pl.pallas_call(functools.partial(kernel, sizes), out_shape=jax.ShapeDtype...  1.77 us
    unnamed x1, local copies, waits for them, and re-layouts  1.76 us

profile of v2, /device:TPU:0, one launch (start us, length us, event | category | flops | bytes accessed | tf_op | source)
XLA Modules:
  0.0 43.2 jit_solution(7703819342134946233)
XLA Ops:
  0.7 1.8 %copy.11.cells_hbm = bf16[4,128,192]{2,1,0:T(8,128)(2,1)} copy(bf16[4,128,192]{1,2,0:T(8,128)(2,1)} %param.10) | data formatting | bytes 393216 | tf_op args[0]
  2.4 39.1 %shard_map.100 = bf16[4,128,192]{2,1,0:T(8,128)(2,1)} custom-call(s32[4]{0:T(128)} %counts_ref.1, s32[1]{0:T(128)S(6)} %copy.13.train_ref, f32[3,192]{1,0:T(4,128)} %gain_ref.1, bf16[4,128,192]{2,1,0:T(8,128)(2,1)} %copy.11.cells_hbm, bf16[48,576]{1,0:T(8,128)(2,1)} %fi_hbm.1, bf16[48,192]{1,0:T(8,128)(2,1)} %fo_hbm.1, bf16[48,576]{1,0:T(8,128)(2,1)} %si_hbm.1, ...), custom_call_target="tpu_custom_call" | custom-call | tf_op jit(solution)/shard_map/pallas_call | solution.py:390
  41.5 1.8 %copy.12 = bf16[4,128,192]{1,2,0:T(8,128)(2,1)} copy(bf16[4,128,192]{2,1,0:T(8,128)(2,1)} %shard_map.100) | data formatting | bytes 393216 | tf_op jit(solution)/shard_map/pallas_call | solution.py:390

commit v3 on v2

--- a/solution.py
+++ b/solution.py
@@ -49,16 +49,23 @@
     return jnp.where(column == source(to), 1.0, 0.0).astype(BF16)
 
 
-def reorder(x, count, source, chunk=512):
+def prepare(ref, source, chunk=512):
+    count, depth = ref.shape
+    chunk = min(chunk, count)
+    for start in range(0, count, chunk):
+        ref[start : start + chunk, :] = one_hot(chunk, depth, start, source)
+
+
+def reorder(pick, x, start=0, count=None, chunk=512):
+    count = pick.shape[0] if count is None else count
     chunk = min(chunk, count)
     pieces = [
-        matmul(one_hot(chunk, x.shape[0], start, source), x)
-        for start in range(0, count, chunk)
+        matmul(pick[at : at + chunk, :], x) for at in range(start, start + count, chunk)
     ]
     return pieces[0] if len(pieces) == 1 else jnp.concatenate(pieces, axis=0)
 
 
-def attend(q, k, v, bias):
+def attend(q, k, v, bias, ones):
     length, width = q.shape
     head_size = width // HEADS
     factor = math.log2(math.e) / math.sqrt(head_size)
@@ -67,7 +74,6 @@
     masks = [head_of == h for h in range(HEADS)]
     keys = jnp.concatenate([jnp.where(m, k, zero) for m in masks], axis=0)
     values = jnp.concatenate([jnp.where(m, v, zero) for m in masks], axis=0)
-    ones = jnp.concatenate([jnp.where(m, 1.0, 0.0).astype(BF16) for m in masks], axis=0)
     scores = lax.dot_general(q, keys, (((1,), (1,)), ((), ())), preferred_element_type=F32)
     powers = []
     for h in range(HEADS):
@@ -77,7 +83,13 @@
     return (matmul(weight, values) / matmul(weight, ones)).astype(BF16)
 
 
-def attention_block(x, w_ref, part, qkv_ref, ctx_ref, length, bias_of, gain):
+def head_ones(ref, length):
+    row = lax.broadcasted_iota(jnp.int32, ref.shape, 0) // length
+    lane = lax.broadcasted_iota(jnp.int32, ref.shape, 1) // (ref.shape[1] // HEADS)
+    ref[...] = jnp.where(row == lane, 1.0, 0.0).astype(BF16)
+
+
+def attention_block(x, w_ref, part, qkv_ref, ctx_ref, ones_ref, length, bias_of, gain):
     width = x.shape[1]
     left, right = gathered(w_ref, part), gathered(w_ref, part + 1)
     qk = matmul(x, left).astype(BF16)
@@ -88,7 +100,7 @@
     def one(i):
         rows = pl.ds(pl.multiple_of(i * length, length), length)
         ctx_ref[rows, :] = attend(
-            qkv_ref[0, rows, :], qkv_ref[1, rows, :], qkv_ref[2, rows, :], bias_of(i)
+            qkv_ref[0, rows, :], qkv_ref[1, rows, :], qkv_ref[2, rows, :], bias_of(i), ones_ref[...]
         )
 
     count = x.shape[0] // length
@@ -115,16 +127,24 @@
     hd_hbm,
     out_ref,
     cells_ref,
+    x_ref,
     fi_ref,
     fo_ref,
     si_ref,
     so_ref,
     hu_ref,
     hd_ref,
-    wa,
+    wf,
+    ws,
     wb,
     qkv,
     ctx,
+    pick_send,
+    pick_column,
+    pick_return,
+    pick_row,
+    feature_ones,
+    sample_ones,
     send1,
     recv1,
     send2,
@@ -150,7 +170,7 @@
     side = part // 2
     near = w + 2 - 4 * side
     far_part = part + 2 - 4 * side
-    rows, feats, width = cells_ref.shape
+    rows, width, feats = cells_ref.shape
     local = feats // total
     block = rows * local
     all_rows = rows * total
@@ -187,10 +207,10 @@
     shard = fi_ref.shape[0]
     for load in loads[:4]:
         load.wait()
-    wa[n, 0] = fi_ref[:, :half]
-    wa[n, 1] = jnp.concatenate([fi_ref[:, half:], fo_ref[...]], axis=1)
-    wa[n, 2] = si_ref[:, :half]
-    wa[n, 3] = jnp.concatenate([si_ref[:, half:], so_ref[...]], axis=1)
+    wf[n, 0] = fi_ref[:, :half]
+    wf[n, 1] = jnp.concatenate([fi_ref[:, half:], fo_ref[...]], axis=1)
+    ws[n, 0] = si_ref[:, :half]
+    ws[n, 1] = jnp.concatenate([si_ref[:, half:], so_ref[...]], axis=1)
     for load in loads[4:]:
         load.wait()
     wb[n, 0] = hu_ref[:, :half]
@@ -200,29 +220,59 @@
         top = down[2 * i * shard : (2 * i + 1) * shard]
         low = down[(2 * i + 1) * shard : (2 * i + 2) * shard]
         wb[n, 2 + i] = jnp.concatenate([top, low], axis=1).astype(BF16)
+    for r in range(rows):
+        x_ref[r * feats : (r + 1) * feats, :] = cells_ref[r].astype(F32).T.astype(BF16)
+    part_rows = block // 2
+    part_cells = cells // 2
+
+    def to_send(i):
+        h, k = i // part_cells, i % part_cells
+        d, j, r = k // part_rows, (k % part_rows) // rows, k % rows
+        return r * feats + d * local + h * (local // 2) + j
+
+    def to_column(i):
+        j, s, r = i // all_rows, (i % all_rows) // rows, i % rows
+        return s * part_rows + j * rows + r
+
+    def to_return(i):
+        s, j, r = i // part_rows, (i % part_rows) // rows, i % rows
+        return j * all_rows + s * rows + r
+
+    def to_row(i):
+        r, d, j = i // feats, (i % feats) // local, i % local
+        h = j // (local // 2)
+        return h * part_cells + d * part_rows + (j % (local // 2)) * rows + r
+
+    prepare(pick_send, to_send)
+    prepare(pick_column, to_column)
+    prepare(pick_return, to_return)
+    prepare(pick_row, to_row)
+    head_ones(feature_ones, feats)
+    head_ones(sample_ones, all_rows)
     pl.semaphore_wait(barrier, total - 1)
 
-    weights = (wa, wb)
+    weights = (wf, ws, wb)
+    mine = (core, core, part)
 
     def along(group, step):
         ref = weights[group]
         return pltpu.make_async_remote_copy(
-            src_ref=ref.at[n, part],
-            dst_ref=ref.at[n, part],
+            src_ref=ref.at[n, mine[group]],
+            dst_ref=ref.at[n, mine[group]],
             send_sem=sa.at[group, step],
             recv_sem=ra.at[group, step],
             device_id=(g, w, lax.rem(n + step, narrow)),
             device_id_type=MESH,
         )
 
-    def beside(group, step):
-        ref = weights[group]
+    def beside(step):
+        ref = wb
         owner = lax.rem(n - step + narrow, narrow)
         return pltpu.make_async_remote_copy(
             src_ref=ref.at[owner, part],
             dst_ref=ref.at[owner, part],
-            send_sem=sx.at[group, step],
-            recv_sem=rx.at[group, step],
+            send_sem=sx.at[step],
+            recv_sem=rx.at[step],
             device_id=(g, near, n),
             device_id_type=MESH,
         )
@@ -230,7 +280,7 @@
     def across(group, far, step):
         ref = weights[group]
         owner = lax.rem(n - step + narrow, narrow)
-        which = far_part if far else part
+        which = far_part if far else mine[group]
         return pltpu.make_async_remote_copy(
             src_ref=ref.at[owner, which],
             dst_ref=ref.at[owner, which],
@@ -241,25 +291,26 @@
         )
 
     steps = range(1, narrow)
-    for group in range(2):
-        for step in steps:
-            along(group, step).start()
+    for step in steps:
+        along(0, step).start()
 
     def forward(group):
         for step in steps:
             along(group, step).wait_recv()
-            beside(group, step).start()
+            if group == 2:
+                beside(step).start()
             across(group, 0, step).start()
 
-    def forward_far(group):
+    def forward_far():
         for step in steps:
-            beside(group, step).wait_recv()
-            across(group, 1, step).start()
+            beside(step).wait_recv()
+            across(2, 1, step).start()
 
     def arrive(group):
         for step in steps:
             across(group, 0, step).wait_recv()
-            across(group, 1, step).wait_recv()
+            if group == 2:
+                across(group, 1, step).wait_recv()
 
     def exchange(send, recv, index):
         recv[me] = send[me]
@@ -290,45 +341,37 @@
         return both[:, :width], both[:, width:]
 
     forward(0)
-    forward_far(0)
+    for group in (1, 2):
+        for step in steps:
+            along(group, step).start()
     arrive(0)
-    x = cells_ref[...].reshape(cells, width)
+    x = x_ref[...]
     keys = lax.broadcasted_iota(jnp.int32, (1, feats), 1)
 
     def row_bias(i):
         return jnp.where(keys < counts_ref[i], 0.0, -1e30)
 
-    first = attention_block(x, wa, 0, qkv, ctx, feats, row_bias, gain_ref[0:1, :])
-
-    part_rows = block // 2
-    part_cells = cells // 2
-
-    def to_send(i):
-        h, k = i // part_cells, i % part_cells
-        d, j, r = k // part_rows, (k % part_rows) // rows, k % rows
-        return r * feats + d * local + h * (local // 2) + j
-
-    picked = reorder(first, cells, to_send)
+    first = attention_block(x, wf, 0, qkv, ctx, feature_ones, feats, row_bias, gain_ref[0:1, :])
+
+    picked = reorder(pick_send, first)
     send1[...] = packed(picked[:part_cells], picked[part_cells:])
     exchange(send1, recv1, 0)
     forward(1)
-    forward_far(1)
+    forward(2)
+    forward_far()
+    arrive(1)
     exchanged(send1, recv1, 0)
 
-    def to_column(i):
-        j, s, r = i // all_rows, (i % all_rows) // rows, i % rows
-        return s * part_rows + j * rows + r
-
     y = jnp.concatenate(
-        [reorder(v, part_cells, to_column).astype(BF16) for v in unpacked(recv1)], axis=0
+        [reorder(pick_column, v).astype(BF16) for v in unpacked(recv1)], axis=0
     )
     samples = lax.broadcasted_iota(jnp.int32, (1, all_rows), 1)
     sample_bias = jnp.where(samples < train_ref[0], 0.0, -1e30)
     second = attention_block(
-        y, wa, 2, qkv, ctx, all_rows, lambda i: sample_bias, gain_ref[1:2, :]
+        y, ws, 0, qkv, ctx, sample_ones, all_rows, lambda i: sample_bias, gain_ref[1:2, :]
     )
 
-    arrive(1)
+    arrive(2)
     ctx[...] = second
     tile = min(512, cells)
     up = [gathered(wb, c) for c in range(2)]
@@ -349,63 +392,69 @@
     else:
         pl.loop(0, cells // tile)(feed)
 
-    def to_return(i):
-        s, j, r = i // part_rows, (i % part_rows) // rows, i % rows
-        return j * all_rows + s * rows + r
-
     send2[...] = packed(
-        reorder(ctx[:part_cells, :], part_cells, to_return),
-        reorder(ctx[part_cells:, :], part_cells, to_return),
+        reorder(pick_return, ctx[:part_cells, :]),
+        reorder(pick_return, ctx[part_cells:, :]),
     )
     exchange(send2, recv2, 2)
-    for group in range(2):
-        for step in steps:
+    for step in steps:
+        for group in range(3):
             along(group, step).wait_send()
-            beside(group, step).wait_send()
             across(group, 0, step).wait_send()
-            across(group, 1, step).wait_send()
+        beside(step).wait_send()
+        across(2, 1, step).wait_send()
     exchanged(send2, recv2, 2)
 
-    def to_row(i):
-        r, d, j = i // feats, (i % feats) // local, i % local
-        h = j // (local // 2)
-        return h * part_cells + d * part_rows + (j % (local // 2)) * rows + r
-
     landed = jnp.concatenate(unpacked(recv2), axis=0)
-    out_ref[...] = reorder(landed, cells, to_row).astype(BF16).reshape(rows, feats, width)
+    for r in range(rows):
+        ordered = reorder(pick_row, landed, r * feats, feats)
+        out_ref[r] = ordered.T.astype(BF16)
 
 
 def body(sizes, cells, counts, train, gain, fi, fo, si, so, hu, hd):
     wide, narrow = sizes
     total = wide * narrow
-    rows, feats, width = cells.shape
+    cells = jnp.swapaxes(cells, 1, 2)
+    rows, width, feats = cells.shape
     block = rows * (feats // total)
     shard = fi.shape[0]
     vmem = pl.BlockSpec(memory_space=pltpu.VMEM)
     smem = pl.BlockSpec(memory_space=pltpu.SMEM)
+    whole = pltpu.VMEM((rows * feats, rows * feats), BF16)
+    half = pltpu.VMEM((rows * feats // 2, rows * feats // 2), BF16)
     blocks = pltpu.VMEM((total, block // 2, 2 * width), BF16)
-    sems = pltpu.SemaphoreType.DMA((2, narrow))
-    far_sems = pltpu.SemaphoreType.DMA((2, 2, narrow))
-    weight = pltpu.VMEM((narrow, 4, shard, 2 * width), BF16)
-    return pl.pallas_call(
+    sems = pltpu.SemaphoreType.DMA((3, narrow))
+    near_sems = pltpu.SemaphoreType.DMA((narrow,))
+    far_sems = pltpu.SemaphoreType.DMA((3, 2, narrow))
+    weight = pltpu.VMEM((narrow, 2, shard, 2 * width), BF16)
+    out = pl.pallas_call(
         functools.partial(kernel, sizes),
         out_shape=jax.ShapeDtypeStruct(cells.shape, BF16),
         in_specs=[smem, smem, vmem] + [pl.BlockSpec(memory_space=pl.ANY)] * 7,
         out_specs=vmem,
         scratch_shapes=[
-            *[pltpu.VMEM(a.shape, BF16) for a in (cells, fi, fo, si, so, hu, hd)],
+            pltpu.VMEM(cells.shape, BF16),
+            pltpu.VMEM((rows * feats, width), BF16),
+            *[pltpu.VMEM(a.shape, BF16) for a in (fi, fo, si, so, hu, hd)],
             weight,
             weight,
+            pltpu.VMEM((narrow, 4, shard, 2 * width), BF16),
             pltpu.VMEM((3, rows * feats, width), BF16),
             pltpu.VMEM((rows * feats, width), BF16),
+            whole,
+            half,
+            half,
+            whole,
+            pltpu.VMEM((HEADS * feats, width), BF16),
+            pltpu.VMEM((HEADS * rows * total, width), BF16),
             blocks,
             blocks,
             blocks,
             blocks,
             sems,
             sems,
-            sems,
-            sems,
+            near_sems,
+            near_sems,
             far_sems,
             far_sems,
             pltpu.SemaphoreType.DMA((4,)),
@@ -415,6 +464,7 @@
             collective_id=0, has_side_effects=True, vmem_limit_bytes=56 << 20
         ),
     )(counts, train, gain, cells, fi, fo, si, so, hu, hd)
+    return jnp.swapaxes(out, 1, 2)
 
 
 def solution(mesh):

time: 43.5 us -> 40.2 us (0.924)
  local copies, waits for them, and re-layouts: 3.52 us -> 1.62 us
  Pallas kernels: 39.1 us -> 37.7 us
    pallas_call x1 -> x0, local copies, waits for them, and re-layouts: 1.77 us -> none  [body(): pl.pallas_call(functools.partial(kernel, sizes), out_shape=jax.ShapeDtype...]
    pallas_call x1, Pallas kernels: 39.1 us -> 37.7 us  [body(): pl.pallas_call(functools.partial(kernel, sizes), out_shape=jax.ShapeDtype...]
where the time goes in v3:
time: 40.2 us; the launch traced here: 40 us
  Pallas kernels  37.7 us (94%)
  local copies, waits for them, and re-layouts  1.62 us (4%)
  between operations  0.66 us (2%)
    pallas_call x1, Pallas kernels, body(): pl.pallas_call(functools.partial(kernel, sizes), out_shape=jax.ShapeDtype...  37.7 us
    unnamed x1, local copies, waits for them, and re-layouts  1.62 us

profile of v3, /device:TPU:0, one launch (start us, length us, event | category | flops | bytes accessed | tf_op | source)
XLA Modules:
  0.0 40.0 jit_solution(5132173682672501942)
XLA Ops:
  0.7 37.7 %shard_map.100 = bf16[4,192,128]{2,1,0:T(8,128)(2,1)} custom-call(s32[4]{0:T(128)} %counts_ref.1, s32[1]{0:T(128)S(6)} %copy.12.train_ref, f32[3,192]{1,0:T(4,128)} %gain_ref.1, bf16[4,192,128]{2,1,0:T(8,128)(2,1)} %bitcast.3, bf16[48,576]{1,0:T(8,128)(2,1)} %fi_hbm.1, bf16[48,192]{1,0:T(8,128)(2,1)} %fo_hbm.1, bf16[48,576]{1,0:T(8,128)(2,1)} %si_hbm.1, ...), custom_call_target="tpu_custom_call" | custom-call | tf_op jit(solution)/shard_map/pallas_call | solution.py:430
  38.3 1.6 %copy.13 = bf16[4,128,192]{1,2,0:T(8,128)(2,1)} copy(bf16[4,128,192]{1,2,0:T(8,128)(2,1)} %bitcast.2) | data formatting | bytes 393216

commit v4 on v3

--- a/solution.py
+++ b/solution.py
@@ -315,7 +315,7 @@
     def exchange(send, recv, index):
         recv[me] = send[me]
 
-        @pl.loop(1, total)
+        @pl.loop(1, total, unroll=True)
         def _(step):
             d = lax.rem(me + step, total)
             pltpu.make_async_remote_copy(

time: 40.2 us -> 40.1 us (level)
  no operation moved by 1% of the time
where the time goes in v4:
time: 40.1 us; the launch traced here: 39.9 us
  Pallas kernels  37.7 us (94%)
  local copies, waits for them, and re-layouts  1.62 us (4%)
  between operations  0.66 us (2%)
    pallas_call x1, Pallas kernels, body(): pl.pallas_call(functools.partial(kernel, sizes), out_shape=jax.ShapeDtype...  37.7 us
    unnamed x1, local copies, waits for them, and re-layouts  1.62 us

profile of v4, /device:TPU:0, one launch (start us, length us, event | category | flops | bytes accessed | tf_op | source)
XLA Modules:
  0.0 39.9 jit_solution(7906213147676735012)
XLA Ops:
  0.7 37.7 %shard_map.100 = bf16[4,192,128]{2,1,0:T(8,128)(2,1)} custom-call(s32[4]{0:T(128)} %counts_ref.1, s32[1]{0:T(128)S(6)} %copy.12.train_ref, f32[3,192]{1,0:T(4,128)} %gain_ref.1, bf16[4,192,128]{2,1,0:T(8,128)(2,1)} %bitcast.3, bf16[48,576]{1,0:T(8,128)(2,1)} %fi_hbm.1, bf16[48,192]{1,0:T(8,128)(2,1)} %fo_hbm.1, bf16[48,576]{1,0:T(8,128)(2,1)} %si_hbm.1, ...), custom_call_target="tpu_custom_call" | custom-call | tf_op jit(solution)/shard_map/pallas_call | solution.py:430
  38.3 1.6 %copy.13 = bf16[4,128,192]{1,2,0:T(8,128)(2,1)} copy(bf16[4,128,192]{1,2,0:T(8,128)(2,1)} %bitcast.2) | data formatting | bytes 393216
